TPU v7x, 32 devices: a whole 2x2x4 slice. The times are simulated.
32 devices in a mesh: row: 8 (over z, core), col: 4 (over y, x).
Axes of the slice: x: 2, y: 2, z: 4, core: 2. Of those that a mesh axis runs over, the one named last changes fastest.
Arguments:
- matrix_tiles: float32 [10, 8, 128, 20, 4, 128], P(None, 'row', None, None, 'col'), may hold values from -60715.73 to 60715.73
Outputs:
- reduced: float32 [10, 8, 128, 20, 4, 128], P(None, 'row', None, None, 'col')
All inputs are finite; a program needn't handle non-finite values.
Results may differ from a plain program's by a relative error of at most 0.0003.
Values sent between devices are 32-bit elements; how exact they have to be, the bound alone decides.
A program may use at most 128 MiB of HBM per device.

v0:
```python
import jax
import jax.numpy as jnp
from jax import lax
from jax.sharding import PartitionSpec as P

BAND = 256
PANELS = 2


def from_root(shard, axis, root):
    mine = lax.axis_index(axis) == root
    return lax.psum(jnp.where(mine, shard, jnp.zeros_like(shard)), axis)


def multiply(first_matrix, second_matrix):
    return jnp.dot(
        first_matrix,
        second_matrix,
        precision=lax.Precision.HIGHEST,
        preferred_element_type=first_matrix.dtype,
    )


def transposed_left(first_matrix, second_matrix):
    return lax.dot_general(
        first_matrix,
        second_matrix,
        (((0,), (0,)), ((), ())),
        precision=lax.Precision.HIGHEST,
        preferred_element_type=first_matrix.dtype,
    )


def transposed_right(first_matrix, second_matrix):
    return lax.dot_general(
        first_matrix,
        second_matrix,
        (((1,), (1,)), ((), ())),
        precision=lax.Precision.HIGHEST,
        preferred_element_type=first_matrix.dtype,
    )


def lower_inverse(matrix):
    factor = jnp.linalg.cholesky(matrix)
    identity = jnp.eye(matrix.shape[0], dtype=matrix.dtype)
    return lax.linalg.triangular_solve(factor, identity, left_side=True, lower=True)


def reflector_factors(gram_matrix, top_panel):
    inverse = lower_inverse(gram_matrix)
    top_basis = transposed_right(top_panel, inverse)
    sign_values = jnp.where(jnp.diagonal(top_basis) >= 0, -1.0, 1.0).astype(top_basis.dtype)
    shifted = top_basis - jnp.diag(sign_values)
    outer_inverse = lower_inverse(transposed_left(shifted, shifted))
    kernel = transposed_left(outer_inverse, outer_inverse)
    transform = -sign_values[:, None] * multiply(shifted, kernel)
    return (inverse, sign_values, transform)


def mirror_order(pieces, block_rows, tile_size):
    stacked = jnp.stack(pieces, 0)
    stacked = stacked.reshape(len(pieces), block_rows, tile_size, stacked.shape[-1])
    return stacked.transpose(1, 0, 2, 3).reshape(-1, stacked.shape[-1])


def on_device(matrix_tiles):
    tile_shape = matrix_tiles.shape
    block_rows = tile_shape[0]
    tile_size = tile_shape[2]
    block_cols = tile_shape[3]
    row_count = block_rows * tile_size
    col_count = block_cols * tile_size
    local_block = matrix_tiles.reshape(row_count, col_count)
    row_devices = lax.axis_size("row")
    col_devices = lax.axis_size("col")
    row_ratio = row_devices // col_devices
    row_index = lax.axis_index("row")
    col_index = lax.axis_index("col")
    positions = jnp.arange(row_count, dtype=jnp.int32)
    global_rows = (
        positions // tile_size * row_devices + row_index
    ) * tile_size + positions % tile_size
    band_columns = jnp.arange(BAND, dtype=jnp.int32)
    panel_tiles = BAND // tile_size
    for panel_index in range(PANELS):
        panel_start = panel_index * BAND
        below_start = panel_start + BAND
        pieces = []
        for offset in range(panel_tiles):
            column_tile = panel_start // tile_size + offset
            local_tile = column_tile // col_devices
            source = local_block[:, local_tile * tile_size : (local_tile + 1) * tile_size]
            pieces.append(from_root(source, "col", column_tile % col_devices))
        panel_rows = jnp.concatenate(pieces, 1)
        panel_rows = jnp.where((global_rows >= below_start)[:, None], panel_rows, 0.0)
        partial_gram = transposed_left(panel_rows, panel_rows)
        gram_matrix = lax.psum(partial_gram, "row")
        blocks = []
        for offset in range(panel_tiles):
            row_tile = below_start // tile_size + offset
            local_tile = row_tile // row_devices
            source = panel_rows[local_tile * tile_size : (local_tile + 1) * tile_size]
            blocks.append(from_root(source, "row", row_tile % row_devices))
        top_panel = jnp.concatenate(blocks, 0)
        inverse, sign_values, transform = reflector_factors(gram_matrix, top_panel)
        sign_places = (global_rows[:, None] - below_start == band_columns[None, :]).astype(
            local_block.dtype
        )
        vec_rows = transposed_right(panel_rows, inverse) - sign_places * sign_values[None, :]
        pieces = []
        for part_index in range(row_ratio):
            pieces.append(from_root(vec_rows, "row", col_index + col_devices * part_index))
        vec_cols = mirror_order(pieces, block_rows, tile_size)
        summed_rows = lax.psum(multiply(local_block, vec_cols), "col")
        applied = multiply(summed_rows, transform)
        inner_term = multiply(transform.T, lax.psum(transposed_left(vec_rows, applied), "row"))
        update_rows = applied - 0.5 * multiply(vec_rows, inner_term)
        column_part = transposed_left(local_block, vec_rows)
        summed_cols = lax.psum(column_part, "row")
        update_cols = multiply(summed_cols, transform) - 0.5 * multiply(vec_cols, inner_term)
        left_factor = jnp.concatenate([vec_rows, update_rows], 1)
        right_factor = jnp.concatenate([update_cols, vec_cols], 1)
        local_block = local_block - transposed_right(left_factor, right_factor)
    return local_block.reshape(tile_shape)


def solution(mesh):
    return jax.shard_map(
        on_device,
        mesh=mesh,
        in_specs=(P(None, "row", None, None, "col", None),),
        out_specs=P(None, "row", None, None, "col", None),
        check_vma=False,
    )
```

profile of v0, /device:TPU:0, one launch (start us, length us, event | category | flops | bytes accessed | tf_op | source)
XLA Modules:
  0.0 1142.7 jit_solution(3032368912725932266)
XLA Ops:
  6.5 102.2 %reduce.8 = f32[10,128,20,128]{3,2,1,0:T(8,128)} reduce(f32[10,1,128,20,1,128]{5,4,3,2,1,0:T(1,128)} %param.4, f32[]{:T(128)} %constant.208), dimensions={1,4}, to_apply=%param.4.reduce_sub_computation | reduce | bytes 26214404 | tf_op args[0]
  108.8 13.6 %copy.28 = f32[160,8,20,128]{3,1,2,0:T(8,128)} copy(f32[160,8,20,128]{3,2,1,0:T(8,128)} %bitcast.198) | data formatting | bytes 26214400
  122.4 2.2 slice_select_fusion.3
  124.7 59.2 %all-reduce.38.cloned.1.call-done = (f32[1280,128]{1,0:T(8,128)}, f32[1280,128]{1,0:T(8,128)}) async-done(((f32[1280,128]{1,0:T(8,128)}, f32[1280,128]{1,0:T(8,128)}), (f32[1280,128]{1,0:T(8,128)}, f32[1280,128]{1,0:T(8,128)})) %all-reduce.38.cloned.1.call-update) | async-done | bytes 1310736 | tf_op jit(solution)/shard_map/psum | solution.py:12
  183.9 1.5 maximum_select_fusion
  185.4 3.0 fusion.104
  189.5 56.5 %all-reduce.34.cloned.1.call-done = (f32[128,256]{1,0:T(8,128)}, f32[128,256]{1,0:T(8,128)}, f32[256,256]{0,1:T(8,128)}) async-done(((f32[128,256]{1,0:T(8,128)}, f32[128,256]{1,0:T(8,128)}, f32[256,256]{0,1:T(8,128)}), (f32[128,256]{1,0:T(8,128)}, f32[128,256]{1,0:T(8,128)}, f32[256,256]{0,1:T(8,128)})) %all-reduce.34.cloned.1.call-update) | async-done | bytes 524304 | tf_op jit(solution)/shard_map/psum | solution.py:12
  248.1 11.7 %cholesky.214 = f32[128,128]{1,0:T(8,128)S(1)} custom-call(f32[128,128]{1,0:T(8,128)S(1)} %cholesky.346), custom_call_target="Cholesky" | custom-call | tf_op jit(solution)/shard_map/jit(cholesky)/cholesky | solution.py:45
  259.9 9.8 custom-call.21
  270.2 11.7 %cholesky.231 = f32[128,128]{1,0:T(8,128)S(1)} custom-call(f32[128,128]{1,0:T(8,128)S(1)} %convolution_subtract_fusion.11), custom_call_target="Cholesky" | custom-call | tf_op jit(solution)/shard_map/jit(cholesky)/cholesky | solution.py:45
  284.0 4.1 while.8
  288.1 19.7 %custom-call.22 = f32[2,128,128]{1,2,0:T(8,128)S(1)} custom-call(f32[2,128,128]{2,1,0:T(8,128)S(1)} %get-tuple-element.33), custom_call_target="InvertDiagBlocksLowerTriangular" | custom-call | tf_op jit(solution)/shard_map/triangular_solve/custom-call.0 | solution.py:47
  309.1 11.1 gather_fusion
  321.1 11.7 %cholesky.248 = f32[128,128]{1,0:T(8,128)S(1)} custom-call(f32[128,128]{1,0:T(8,128)S(1)} %cholesky.349), custom_call_target="Cholesky" | custom-call | tf_op jit(solution)/shard_map/jit(cholesky)/cholesky | solution.py:45
  332.9 9.8 custom-call.23
  343.2 11.7 %cholesky.265 = f32[128,128]{1,0:T(8,128)S(1)} custom-call(f32[128,128]{1,0:T(8,128)S(1)} %convolution_subtract_fusion.10), custom_call_target="Cholesky" | custom-call | tf_op jit(solution)/shard_map/jit(cholesky)/cholesky | solution.py:45
  357.6 3.6 broadcast_select_fusion.3
  361.3 4.1 while.9
  365.4 19.7 %custom-call.24 = f32[2,128,128]{1,2,0:T(8,128)S(1)} custom-call(f32[2,128,128]{2,1,0:T(8,128)S(1)} %get-tuple-element.34), custom_call_target="InvertDiagBlocksLowerTriangular" | custom-call | tf_op jit(solution)/shard_map/triangular_solve/custom-call.0 | solution.py:47
  385.7 44.1 %all-reduce.32.cloned.1.call-done = (f32[1,10,128,256]{3,2,0,1:T(8,128)}, f32[1,10,128,256]{3,2,0,1:T(8,128)}) async-done(((f32[1,10,128,256]{3,2,0,1:T(8,128)}, f32[1,10,128,256]{3,2,0,1:T(8,128)}), (f32[1,10,128,256]{3,2,0,1:T(8,128)}, f32[1,10,128,256]{3,2,0,1:T(8,128)})) %all-reduce.32.cloned.1.call-update) | async-done | bytes 2621456 | tf_op jit(solution)/shard_map/psum | solution.py:12
  429.8 2.0 pad_maximum_fusion
  431.7 25.7 %convolution_bitcast_fusion.1 = f32[1280,256]{0,1:T(8,128)} fusion(f32[2560,256]{1,0:T(8,128)S(1)} %bitcast.202, f32[1280,2560]{1,0:T(8,128)} %bitcast.193), kind=kOutput, calls=%fused_computation.30 | convolution fusion | flops 10066329600 | bytes 17039360 | tf_op jit(solution)/shard_map/dot_general | solution.py:16
  458.9 15.8 %convolution_bitcast_fusion = f32[2560,256]{0,1:T(8,128)} fusion(f32[1280,256]{1,0:T(8,128)S(1)} %copy-done.4, f32[1280,2560]{1,0:T(8,128)} %bitcast.194), kind=kOutput, calls=%fused_computation.23 | convolution fusion | flops 10066329600 | bytes 17039360 | tf_op jit(solution)/shard_map/dot_general | solution.py:25
  474.8 38.4 %all-reduce.20.cloned.1.call-done = f32[1280,256]{0,1:T(8,128)} async-done(((f32[1280,256]{0,1:T(8,128)}), f32[1280,256]{0,1:T(8,128)}) %all-reduce.20.cloned.1.call-update) | async-done | bytes 1310736 | tf_op jit(solution)/shard_map/psum | solution.py:115
  513.2 2.8 fusion.105
  517.1 3.0 fusion.106
  520.4 2.8 copy.16
  523.2 69.6 %all-reduce.30.cloned.1.call-done = (f32[2560,256]{0,1:T(8,128)}, f32[256,256]{1,0:T(8,128)}) async-done(((f32[2560,256]{0,1:T(8,128)}, f32[256,256]{1,0:T(8,128)}), (f32[2560,256]{0,1:T(8,128)}, f32[256,256]{1,0:T(8,128)})) %all-reduce.30.cloned.1.call-update) | async-done | bytes 2883600 | tf_op jit(solution)/shard_map/psum | solution.py:120
  592.8 1.5 fusion.107
  594.4 6.1 fusion.108
  601.7 2.2 fusion.7
  604.0 24.8 %convolution_subtract_fusion.1 = f32[1280,2560]{1,0:T(8,128)S(1)} fusion(f32[1280,2560]{1,0:T(8,128)} %bitcast.195, f32[2560,256]{1,0:T(8,128)S(1)} %bitcast.204, f32[2560,256]{1,0:T(8,128)S(1)} %fusion.7, f32[1280,256]{1,0:T(8,128)S(1)} %fusion.9, f32[1280,256]{1,0:T(8,128)S(1)} %copy-done.6), kind=kOutput, calls=%fused_computation.11 | convolution fusion | flops 20137902080 | bytes 34078720 | tf_op jit(solution)/shard_map/dot_general | solution.py:35
  628.8 4.9 copy-done
  635.0 56.0 %all-reduce.36.cloned.1.call-done = (f32[1280,128]{1,0:T(8,128)}, f32[1280,128]{1,0:T(8,128)}) async-done(((f32[1280,128]{1,0:T(8,128)}, f32[1280,128]{1,0:T(8,128)}), (f32[1280,128]{1,0:T(8,128)}, f32[1280,128]{1,0:T(8,128)})) %all-reduce.36.cloned.1.call-update) | async-done | bytes 1310736 | tf_op jit(solution)/shard_map/psum | solution.py:12
  690.9 1.5 maximum_select_fusion.1
  692.5 3.0 fusion.109
  696.5 56.6 %all-reduce.28.cloned.1.call-done = (f32[128,256]{1,0:T(8,128)}, f32[128,256]{1,0:T(8,128)}, f32[256,256]{0,1:T(8,128)}) async-done(((f32[128,256]{1,0:T(8,128)}, f32[128,256]{1,0:T(8,128)}, f32[256,256]{0,1:T(8,128)}), (f32[128,256]{1,0:T(8,128)}, f32[128,256]{1,0:T(8,128)}, f32[256,256]{0,1:T(8,128)})) %all-reduce.28.cloned.1.call-update) | async-done | bytes 524304 | tf_op jit(solution)/shard_map/psum | solution.py:12
  755.2 11.7 %cholesky.282 = f32[128,128]{1,0:T(8,128)S(1)} custom-call(f32[128,128]{1,0:T(8,128)S(1)} %cholesky.352), custom_call_target="Cholesky" | custom-call | tf_op jit(solution)/shard_map/jit(cholesky)/cholesky | solution.py:45
  767.0 9.8 custom-call.25
  777.3 11.7 %cholesky.299 = f32[128,128]{1,0:T(8,128)S(1)} custom-call(f32[128,128]{1,0:T(8,128)S(1)} %convolution_subtract_fusion.9), custom_call_target="Cholesky" | custom-call | tf_op jit(solution)/shard_map/jit(cholesky)/cholesky | solution.py:45
  791.7 4.1 while.10
  795.8 19.7 %custom-call.26 = f32[2,128,128]{1,2,0:T(8,128)S(1)} custom-call(f32[2,128,128]{2,1,0:T(8,128)S(1)} %get-tuple-element.35), custom_call_target="InvertDiagBlocksLowerTriangular" | custom-call | tf_op jit(solution)/shard_map/triangular_solve/custom-call.0 | solution.py:47
  816.8 2.6 gather_fusion.1
  820.2 11.7 %cholesky.316 = f32[128,128]{1,0:T(8,128)S(1)} custom-call(f32[128,128]{1,0:T(8,128)S(1)} %cholesky.355), custom_call_target="Cholesky" | custom-call | tf_op jit(solution)/shard_map/jit(cholesky)/cholesky | solution.py:45
  832.0 9.8 custom-call.27
  842.3 11.7 %cholesky.333 = f32[128,128]{1,0:T(8,128)S(1)} custom-call(f32[128,128]{1,0:T(8,128)S(1)} %convolution_subtract_fusion.8), custom_call_target="Cholesky" | custom-call | tf_op jit(solution)/shard_map/jit(cholesky)/cholesky | solution.py:45
  855.4 3.6 broadcast_select_fusion.1
  860.4 4.2 while.11
  861.1 1.4 bitcast_dynamic-update-slice_fusion.11
  864.6 19.7 %custom-call.28 = f32[2,128,128]{1,2,0:T(8,128)S(1)} custom-call(f32[2,128,128]{2,1,0:T(8,128)S(1)} %get-tuple-element.36), custom_call_target="InvertDiagBlocksLowerTriangular" | custom-call | tf_op jit(solution)/shard_map/triangular_solve/custom-call.0 | solution.py:47
  884.9 44.1 %all-reduce.26.cloned.1.call-done = (f32[1,10,128,256]{3,2,0,1:T(8,128)}, f32[1,10,128,256]{3,2,0,1:T(8,128)}) async-done(((f32[1,10,128,256]{3,2,0,1:T(8,128)}, f32[1,10,128,256]{3,2,0,1:T(8,128)}), (f32[1,10,128,256]{3,2,0,1:T(8,128)}, f32[1,10,128,256]{3,2,0,1:T(8,128)})) %all-reduce.26.cloned.1.call-update) | async-done | bytes 2621456 | tf_op jit(solution)/shard_map/psum | solution.py:12
  929.0 2.0 pad_maximum_fusion.1
  930.9 14.3 %fusion.110 = f32[1280,256]{1,0:T(8,128)} fusion(f32[1280,2560]{1,0:T(8,128)} %copy-done, f32[2560,256]{1,0:T(8,128)S(1)} %bitcast.199), kind=kOutput, calls=%fused_computation.223 | convolution fusion | flops 10066329600 | bytes 17039360 | tf_op jit(solution)/shard_map/dot_general | solution.py:16
  946.6 25.0 %fusion.114 = f32[2560,256]{1,0:T(8,128)} fusion(f32[1280,2560]{1,0:T(8,128)} %copy-done, f32[1280,256]{1,0:T(8,128)S(1)} %copy-done.1), kind=kOutput, calls=%fused_computation.227 | convolution fusion | flops 10066329600 | bytes 17039360 | tf_op jit(solution)/shard_map/dot_general | solution.py:25
  971.7 29.2 %all-reduce.22.cloned.1.call-done = f32[1280,256]{1,0:T(8,128)} async-done(((f32[1280,256]{1,0:T(8,128)}), f32[1280,256]{1,0:T(8,128)}) %all-reduce.22.cloned.1.call-update) | async-done | bytes 1310736 | tf_op jit(solution)/shard_map/psum | solution.py:115
  1000.9 2.8 fusion.111
  1004.8 3.0 fusion.112
  1007.8 2.8 copy.22
  1010.6 69.9 %all-reduce.24.cloned.1.call-done = (f32[2560,256]{1,0:T(8,128)}, f32[256,256]{1,0:T(8,128)}) async-done(((f32[2560,256]{1,0:T(8,128)}, f32[256,256]{1,0:T(8,128)}), (f32[2560,256]{1,0:T(8,128)}, f32[256,256]{1,0:T(8,128)})) %all-reduce.24.cloned.1.call-update) | async-done | bytes 2883600 | tf_op jit(solution)/shard_map/psum | solution.py:120
  1080.5 1.5 fusion.113
  1082.1 4.2 fusion.115
  1087.5 2.3 fusion.6
  1089.8 25.8 %convolution_subtract_fusion = f32[1280,2560]{1,0:T(8,128)} fusion(f32[1280,2560]{1,0:T(8,128)} %copy-done, f32[2560,256]{1,0:T(8,128)S(1)} %bitcast.201, f32[2560,256]{1,0:T(8,128)S(1)} %fusion.6, f32[1280,256]{1,0:T(8,128)S(1)} %fusion.8, f32[1280,256]{1,0:T(8,128)S(1)} %copy-done.3), kind=kOutput, calls=%fused_computation.10 | convolution fusion | flops 20137902080 | bytes 34078720 | tf_op jit(solution)/shard_map/dot_general | solution.py:35
  1115.6 19.9 %reshape.157 = f32[10,1,128,20,1,128]{5,4,3,2,1,0:T(1,128)} reshape(f32[1280,2560]{1,0:T(8,128)} %convolution_subtract_fusion) | data formatting | bytes 26214400 | tf_op jit(solution)/shard_map/reshape | solution.py:125
  (154 shorter events, 42.7 us)
Async XLA Ops:
  6.5 177.3 %all-reduce.38.cloned.1.call-start = ((), (), s32[]{:S(2)}) async-start(), calls=%async_computation.9 | async-start | bytes 2621440 | tf_op jit(solution)/shard_map/psum | solution.py:12
  124.6 121.4 %all-reduce.34.cloned.1.call-start = ((), (), s32[]{:S(2)}) async-start(), calls=%async_computation.7 | async-start | bytes 1048576 | tf_op jit(solution)/shard_map/psum | solution.py:12
  189.1 240.6 %all-reduce.32.cloned.1.call-start = ((), (), s32[]{:S(2)}) async-start(), calls=%async_computation.6 | async-start | bytes 5242880 | tf_op jit(solution)/shard_map/psum | solution.py:12
  281.9 26.7 %copy-start.11 = (f32[128,256]{1,0:T(8,128)S(1)}, f32[128,256]{1,0:T(8,128)}, u32[]{:S(2)}) copy-start(f32[128,256]{1,0:T(8,128)} %get-tuple-element.80) | copy-start | bytes 393220
  281.9 26.7 %copy-start.12 = (f32[128,256]{1,0:T(8,128)S(1)}, f32[128,256]{1,0:T(8,128)}, u32[]{:S(2)}) copy-start(f32[128,256]{1,0:T(8,128)} %get-tuple-element.81) | copy-start | bytes 393220
  361.2 152.0 %all-reduce.20.cloned.1.call-start = ((), (), s32[]{:S(2)}) async-start(), calls=%async_computation | async-start | bytes 2621440 | tf_op jit(solution)/shard_map/psum | solution.py:115
  457.5 135.3 %all-reduce.30.cloned.1.call-start = ((), (), s32[]{:S(2)}) async-start(), calls=%async_computation.5 | async-start | bytes 5767168 | tf_op jit(solution)/shard_map/psum | solution.py:120
  457.6 1.4 copy-start.4
  513.2 3.9 copy-start.5
  516.0 1.1 copy-start.7
  520.1 170.8 %all-reduce.36.cloned.1.call-start = ((), (), s32[]{:S(2)}) async-start(), calls=%async_computation.8 | async-start | bytes 2621440 | tf_op jit(solution)/shard_map/psum | solution.py:12
  594.3 6.2 copy-start.6
  594.4 6.2 copy-start.9
  628.8 5.0 copy-start
  634.9 118.2 %all-reduce.28.cloned.1.call-start = ((), (), s32[]{:S(2)}) async-start(), calls=%async_computation.4 | async-start | bytes 1048576 | tf_op jit(solution)/shard_map/psum | solution.py:12
  696.2 232.7 %all-reduce.26.cloned.1.call-start = ((), (), s32[]{:S(2)}) async-start(), calls=%async_computation.3 | async-start | bytes 5242880 | tf_op jit(solution)/shard_map/psum | solution.py:12
  789.0 27.3 %copy-start.13 = (f32[128,256]{1,0:T(8,128)S(1)}, f32[128,256]{1,0:T(8,128)}, u32[]{:S(2)}) copy-start(f32[128,256]{1,0:T(8,128)} %get-tuple-element.73) | copy-start | bytes 393220
  789.0 27.3 %copy-start.14 = (f32[128,256]{1,0:T(8,128)S(1)}, f32[128,256]{1,0:T(8,128)}, u32[]{:S(2)}) copy-start(f32[128,256]{1,0:T(8,128)} %get-tuple-element.74) | copy-start | bytes 393220
  860.3 140.5 %all-reduce.22.cloned.1.call-start = ((), (), s32[]{:S(2)}) async-start(), calls=%async_computation.1 | async-start | bytes 2621440 | tf_op jit(solution)/shard_map/psum | solution.py:115
  945.2 135.3 %all-reduce.24.cloned.1.call-start = ((), (), s32[]{:S(2)}) async-start(), calls=%async_computation.2 | async-start | bytes 5767168 | tf_op jit(solution)/shard_map/psum | solution.py:120
  945.3 1.4 copy-start.1
  1000.9 3.9 copy-start.2
  1003.7 1.1 copy-start.8
  1082.0 4.2 copy-start.3
  1082.0 4.2 copy-start.10
Sparse Core Ops, SparseCore 0:
  124.7 59.0 all-reduce.37
  189.3 56.7 all-reduce.33
  361.3 68.3 all-reduce.31
  457.6 55.5 all-reduce.19
  520.3 72.4 all-reduce.29
  635.0 55.8 all-reduce.35
  696.3 56.7 all-reduce.27
  860.5 68.4 all-reduce.25
  945.3 55.5 all-reduce.21
  1008.0 72.4 all-reduce.23
where the time goes:
time: 1150 us; the launch traced here: 1140 us
  waiting for transfers between devices  524 us (46%)
  other arithmetic  333 us (29%)
  matrix products  186 us (16%)
  local copies, waits for them, and re-layouts  78.6 us (7%)
  between operations  19.9 us (2%)
    psum x6, waiting for transfers between devices, from_root(): return lax.psum(jnp.where(mine, shard, jnp.zeros_like(shard)), axis)  316 us
    psum x2, waiting for transfers between devices, on_device(): summed_cols = lax.psum(column_part, 'row')  139 us
    another operation x27, other arithmetic, lower_inverse(): factor = jnp.linalg.cholesky(matrix)  138 us
    unnamed x1, other arithmetic  102 us
    another operation x9, other arithmetic, lower_inverse(): lax.linalg.triangular_solve(factor, identity, left_side=True, lower=True)  78.8 us
    psum x2, waiting for transfers between devices, on_device(): summed_rows = lax.psum(multiply(local_block, vec_cols), 'col')  67.6 us
    dot_general x14, matrix products, multiply(): jnp.dot(first_matrix, second_matrix, precision=lax.Precision.HIGHEST, pre...  66.7 us
    dot_general x6, matrix products, transposed_right(): lax.dot_general(first_matrix, second_matrix, (((1,), (1,)), ((), ())), pr...  58.7 us
  transfers between devices with their start and end apart: 10, of which 10 were waited for; matrix products, arithmetic and copies ran while one was open for 9% of the time, Pallas kernels for 0%

commit v1 on v0

--- a/solution.py
+++ b/solution.py
@@ -117,7 +117,11 @@
         inner_term = multiply(transform.T, lax.psum(transposed_left(vec_rows, applied), "row"))
         update_rows = applied - 0.5 * multiply(vec_rows, inner_term)
         column_part = transposed_left(local_block, vec_rows)
-        summed_cols = lax.psum(column_part, "row")
+        summed_cols = column_part
+        for hop in (1, 2, 4):
+            summed_cols = summed_cols + lax.ppermute(
+                summed_cols, "row", [(dev, dev ^ hop) for dev in range(8)]
+            )
         update_cols = multiply(summed_cols, transform) - 0.5 * multiply(vec_cols, inner_term)
         left_factor = jnp.concatenate([vec_rows, update_rows], 1)
         right_factor = jnp.concatenate([update_cols, vec_cols], 1)

time: 1150 us -> 1260 us (1.096)
  waiting for transfers between devices: 524 us -> 603 us
  other arithmetic: 333 us -> 355 us
    psum x2, waiting for transfers between devices: 139 us -> 229 us  [on_device(): lax.psum(transposed_left(vec_rows, applied), 'row')]
    psum x2, waiting for transfers between devices: 67.6 us -> 44.1 us  [on_device(): summed_rows = lax.psum(multiply(local_block, vec_cols), 'col')]
    add x0 -> x4, other arithmetic: none -> 16.4 us  [on_device(): summed_cols + lax.ppermute(summed_cols, 'row', [(dev, dev ^ hop) for dev...]
    psum x6, waiting for transfers between devices: 316 us -> 330 us  [from_root(): return lax.psum(jnp.where(mine, shard, jnp.zeros_like(shard)), axis)]
  transfers between devices with their start and end apart: 10 -> 16, of which waited for: 10 -> 10; matrix products, arithmetic and copies ran while one was open for 9% -> 18% of each run, Pallas kernels for 0% -> 0%
where the time goes in v1:
time: 1260 us; the launch traced here: 1250 us
  waiting for transfers between devices  603 us (48%)
  other arithmetic  355 us (28%)
  matrix products  189 us (15%)
  local copies, waits for them, and re-layouts  73.9 us (6%)
  between operations  19.5 us (2%)
    psum x6, waiting for transfers between devices, from_root(): return lax.psum(jnp.where(mine, shard, jnp.zeros_like(shard)), axis)  330 us
    psum x2, waiting for transfers between devices, on_device(): lax.psum(transposed_left(vec_rows, applied), 'row')  229 us
    another operation x27, other arithmetic, lower_inverse(): factor = jnp.linalg.cholesky(matrix)  138 us
    unnamed x1, other arithmetic  102 us
    another operation x9, other arithmetic, lower_inverse(): lax.linalg.triangular_solve(factor, identity, left_side=True, lower=True)  82.8 us
    dot_general x14, matrix products, multiply(): jnp.dot(first_matrix, second_matrix, precision=lax.Precision.HIGHEST, pre...  72.5 us
    dot_general x6, matrix products, transposed_right(): lax.dot_general(first_matrix, second_matrix, (((1,), (1,)), ((), ())), pr...  57 us
    dot_general x10, matrix products, transposed_left(): lax.dot_general(first_matrix, second_matrix, (((0,), (0,)), ((), ())), pr...  54 us
  transfers between devices with their start and end apart: 16, of which 10 were waited for; matrix products, arithmetic and copies ran while one was open for 18% of the time, Pallas kernels for 0%

profile of v1, /device:TPU:0, one launch (start us, length us, event | category | flops | bytes accessed | tf_op | source)
XLA Modules:
  0.0 1249.1 jit_solution(12088873547385641688)
XLA Ops:
  6.5 102.2 %reduce.8 = f32[10,128,20,128]{3,2,1,0:T(8,128)} reduce(f32[10,1,128,20,1,128]{5,4,3,2,1,0:T(1,128)} %param.4, f32[]{:T(128)} %constant.208), dimensions={1,4}, to_apply=%param.4.reduce_sub_computation | reduce | bytes 26214404 | tf_op args[0]
  108.8 13.6 %copy.28 = f32[160,8,20,128]{3,1,2,0:T(8,128)} copy(f32[160,8,20,128]{3,2,1,0:T(8,128)} %bitcast.196) | data formatting | bytes 26214400
  122.4 2.2 slice_select_fusion.3
  124.7 59.2 %all-reduce.36.cloned.1.call-done = (f32[1280,128]{1,0:T(8,128)}, f32[1280,128]{1,0:T(8,128)}) async-done(((f32[1280,128]{1,0:T(8,128)}, f32[1280,128]{1,0:T(8,128)}), (f32[1280,128]{1,0:T(8,128)}, f32[1280,128]{1,0:T(8,128)})) %all-reduce.36.cloned.1.call-update) | async-done | bytes 1310736 | tf_op jit(solution)/shard_map/psum | solution.py:12
  185.4 3.0 fusion.104
  189.4 56.6 %all-reduce.32.cloned.1.call-done = (f32[128,256]{1,0:T(8,128)}, f32[128,256]{1,0:T(8,128)}, f32[256,256]{0,1:T(8,128)}) async-done(((f32[128,256]{1,0:T(8,128)}, f32[128,256]{1,0:T(8,128)}, f32[256,256]{0,1:T(8,128)}), (f32[128,256]{1,0:T(8,128)}, f32[128,256]{1,0:T(8,128)}, f32[256,256]{0,1:T(8,128)})) %all-reduce.32.cloned.1.call-update) | async-done | bytes 524304 | tf_op jit(solution)/shard_map/psum | solution.py:12
  248.1 11.7 cholesky.214
  259.9 9.8 custom-call.21
  270.2 11.7 cholesky.231
  284.0 4.1 while.8
  288.2 19.7 %custom-call.22 = f32[2,128,128]{1,2,0:T(8,128)S(1)} custom-call(f32[2,128,128]{2,1,0:T(8,128)S(1)} %get-tuple-element.33), custom_call_target="InvertDiagBlocksLowerTriangular" | custom-call | tf_op jit(solution)/shard_map/triangular_solve/custom-call.0 | solution.py:47
  309.2 2.3 gather_fusion
  311.6 2.9 broadcast_select_fusion.3
  314.4 15.1 %convolution_bitcast_fusion = f32[2560,256]{0,1:T(8,128)S(1)} fusion(f32[1280,256]{1,0:T(8,128)S(1)} %get-tuple-element.125, f32[1280,2560]{1,0:T(8,128)} %bitcast.191), kind=kOutput, calls=%fused_computation.23 | convolution fusion | flops 10066329600 | bytes 17039360 | tf_op jit(solution)/shard_map/dot_general | solution.py:25
  333.3 11.7 cholesky.248
  345.1 9.8 custom-call.23
  355.0 3.8 add.166
  359.9 11.7 cholesky.265
  375.1 50.7 %all-reduce.30.cloned.1.call-done = (f32[1,10,128,256]{3,2,0,1:T(8,128)}, f32[1,10,128,256]{3,2,0,1:T(8,128)}) async-done(((f32[1,10,128,256]{3,2,0,1:T(8,128)}, f32[1,10,128,256]{3,2,0,1:T(8,128)}), (f32[1,10,128,256]{3,2,0,1:T(8,128)}, f32[1,10,128,256]{3,2,0,1:T(8,128)})) %all-reduce.30.cloned.1.call-update) | async-done | bytes 2621456 | tf_op jit(solution)/shard_map/psum | solution.py:12
  427.7 26.0 %convolution_bitcast_fusion.1 = f32[1280,256]{0,1:T(8,128)} fusion(f32[2560,256]{1,0:T(8,128)S(1)} %bitcast.200, f32[1280,2560]{1,0:T(8,128)} %bitcast.192), kind=kOutput, calls=%fused_computation.30 | convolution fusion | flops 10066329600 | bytes 17039360 | tf_op jit(solution)/shard_map/dot_general | solution.py:16
  454.4 4.2 while.9
  459.3 20.5 %custom-call.24 = f32[2,128,128]{1,2,0:T(8,128)S(1)} custom-call(f32[2,128,128]{2,1,0:T(8,128)} %copy-done.16), custom_call_target="InvertDiagBlocksLowerTriangular" | custom-call | tf_op jit(solution)/shard_map/triangular_solve/custom-call.0 | solution.py:47
  479.8 4.4 add.167
  484.2 2.5 collective-permute-start.2
  488.6 21.7 %all-reduce.18.cloned.1.call-done = f32[1280,256]{0,1:T(8,128)} async-done(((f32[1280,256]{0,1:T(8,128)}), f32[1280,256]{0,1:T(8,128)}) %all-reduce.18.cloned.1.call-update) | async-done | bytes 1310736 | tf_op jit(solution)/shard_map/psum | solution.py:115
  510.4 2.8 fusion.105
  514.2 3.0 fusion.106
  517.6 2.9 copy.16
  520.4 114.7 %all-reduce.20.cloned.1.call-done = f32[256,256]{1,0:T(8,128)} async-done(((f32[256,256]{1,0:T(8,128)}), f32[256,256]{1,0:T(8,128)}) %all-reduce.20.cloned.1.call-update) | async-done | bytes 262160 | tf_op jit(solution)/shard_map/psum | solution.py:117
  636.7 2.9 fusion.7
  641.9 6.9 convolution_subtract_fusion.3
  648.8 24.9 %convolution_subtract_fusion.1 = f32[1280,2560]{1,0:T(8,128)S(1)} fusion(f32[1280,2560]{1,0:T(8,128)} %bitcast.193, f32[2560,256]{1,0:T(8,128)S(1)} %bitcast.202, f32[2560,256]{1,0:T(8,128)S(1)} %convolution_subtract_fusion.3, f32[1280,256]{1,0:T(8,128)S(1)} %fusion.7, f32[1280,256]{1,0:T(8,128)S(1)} %copy-done.3), kind=kOutput, calls=%fused_computation.11 | convolution fusion | flops 20137902080 | bytes 34078720 | tf_op jit(solution)/shard_map/dot_general | solution.py:35
  673.7 4.9 copy-done
  679.8 55.5 %all-reduce.34.cloned.1.call-done = (f32[1280,128]{1,0:T(8,128)}, f32[1280,128]{1,0:T(8,128)}) async-done(((f32[1280,128]{1,0:T(8,128)}, f32[1280,128]{1,0:T(8,128)}), (f32[1280,128]{1,0:T(8,128)}, f32[1280,128]{1,0:T(8,128)})) %all-reduce.34.cloned.1.call-update) | async-done | bytes 1310736 | tf_op jit(solution)/shard_map/psum | solution.py:12
  736.9 3.0 fusion.108
  740.9 56.6 %all-reduce.28.cloned.1.call-done = (f32[128,256]{1,0:T(8,128)}, f32[128,256]{1,0:T(8,128)}, f32[256,256]{0,1:T(8,128)}) async-done(((f32[128,256]{1,0:T(8,128)}, f32[128,256]{1,0:T(8,128)}, f32[256,256]{0,1:T(8,128)}), (f32[128,256]{1,0:T(8,128)}, f32[128,256]{1,0:T(8,128)}, f32[256,256]{0,1:T(8,128)})) %all-reduce.28.cloned.1.call-update) | async-done | bytes 524304 | tf_op jit(solution)/shard_map/psum | solution.py:12
  799.6 11.7 cholesky.282
  811.4 9.8 custom-call.25
  821.7 11.7 cholesky.299
  836.1 3.9 while.10
  840.0 19.7 %custom-call.26 = f32[2,128,128]{1,2,0:T(8,128)S(1)} custom-call(f32[2,128,128]{2,1,0:T(8,128)S(1)} %get-tuple-element.35), custom_call_target="InvertDiagBlocksLowerTriangular" | custom-call | tf_op jit(solution)/shard_map/triangular_solve/custom-call.0 | solution.py:47
  861.0 2.3 gather_fusion.1
  863.4 2.9 broadcast_select_fusion.1
  866.2 24.4 %fusion.113 = f32[2560,256]{1,0:T(8,128)S(1)} fusion(f32[1280,2560]{1,0:T(8,128)} %copy-done, f32[1280,256]{1,0:T(8,128)S(1)} %get-tuple-element.130), kind=kOutput, calls=%fused_computation.228 | convolution fusion | flops 10066329600 | bytes 17039360 | tf_op jit(solution)/shard_map/dot_general | solution.py:25
  894.2 11.7 cholesky.316
  905.9 9.8 custom-call.27
  915.8 3.8 add.169
  920.7 11.7 cholesky.333
  935.9 51.2 %all-reduce.26.cloned.1.call-done = (f32[1,10,128,256]{3,2,0,1:T(8,128)}, f32[1,10,128,256]{3,2,0,1:T(8,128)}) async-done(((f32[1,10,128,256]{3,2,0,1:T(8,128)}, f32[1,10,128,256]{3,2,0,1:T(8,128)}), (f32[1,10,128,256]{3,2,0,1:T(8,128)}, f32[1,10,128,256]{3,2,0,1:T(8,128)})) %all-reduce.26.cloned.1.call-update) | async-done | bytes 2621456 | tf_op jit(solution)/shard_map/psum | solution.py:12
  989.1 14.5 %fusion.109 = f32[1280,256]{1,0:T(8,128)} fusion(f32[1280,2560]{1,0:T(8,128)} %copy-done, f32[2560,256]{1,0:T(8,128)S(1)} %bitcast.197), kind=kOutput, calls=%fused_computation.224 | convolution fusion | flops 10066329600 | bytes 17039360 | tf_op jit(solution)/shard_map/dot_general | solution.py:16
  1003.7 4.0 while.11
  1008.4 20.9 %custom-call.28 = f32[2,128,128]{1,2,0:T(8,128)S(1)} custom-call(f32[2,128,128]{2,1,0:T(8,128)} %copy-done.15), custom_call_target="InvertDiagBlocksLowerTriangular" | custom-call | tf_op jit(solution)/shard_map/triangular_solve/custom-call.0 | solution.py:47
  1029.4 4.4 add.170
  1033.8 2.3 collective-permute-start.5
  1038.0 22.3 %all-reduce.22.cloned.1.call-done = f32[1280,256]{1,0:T(8,128)} async-done(((f32[1280,256]{1,0:T(8,128)}), f32[1280,256]{1,0:T(8,128)}) %all-reduce.22.cloned.1.call-update) | async-done | bytes 1310736 | tf_op jit(solution)/shard_map/psum | solution.py:115
  1060.4 2.8 fusion.110
  1064.2 3.0 fusion.111
  1067.2 2.9 copy.22
  1070.1 114.5 %all-reduce.24.cloned.1.call-done = f32[256,256]{1,0:T(8,128)} async-done(((f32[256,256]{1,0:T(8,128)}), f32[256,256]{1,0:T(8,128)}) %all-reduce.24.cloned.1.call-update) | async-done | bytes 262160 | tf_op jit(solution)/shard_map/psum | solution.py:117
  1186.2 2.9 fusion.6
  1189.1 2.3 convolution_multiply_fusion
  1191.4 5.2 convolution_subtract_fusion.2
  1196.6 25.6 %convolution_subtract_fusion = f32[1280,2560]{1,0:T(8,128)} fusion(f32[1280,2560]{1,0:T(8,128)} %copy-done, f32[2560,256]{1,0:T(8,128)S(1)} %bitcast.199, f32[2560,256]{1,0:T(8,128)S(1)} %convolution_subtract_fusion.2, f32[1280,256]{1,0:T(8,128)S(1)} %fusion.6, f32[1280,256]{1,0:T(8,128)S(1)} %copy-done.6), kind=kOutput, calls=%fused_computation.10 | convolution fusion | flops 20137902080 | bytes 34078720 | tf_op jit(solution)/shard_map/dot_general | solution.py:35
  1222.2 19.9 %reshape.157 = f32[10,1,128,20,1,128]{5,4,3,2,1,0:T(1,128)} reshape(f32[1280,2560]{1,0:T(8,128)} %convolution_subtract_fusion) | data formatting | bytes 26214400 | tf_op jit(solution)/shard_map/reshape | solution.py:129
  (186 shorter events, 63.7 us)
Async XLA Ops:
  6.5 177.4 %all-reduce.36.cloned.1.call-start = ((), (), s32[]{:S(2)}) async-start(), calls=%async_computation.9 | async-start | bytes 2621440 | tf_op jit(solution)/shard_map/psum | solution.py:12
  124.6 121.4 %all-reduce.32.cloned.1.call-start = ((), (), s32[]{:S(2)}) async-start(), calls=%async_computation.7 | async-start | bytes 1048576 | tf_op jit(solution)/shard_map/psum | solution.py:12
  189.2 236.6 %all-reduce.30.cloned.1.call-start = ((), (), s32[]{:S(2)}) async-start(), calls=%async_computation.6 | async-start | bytes 5242880 | tf_op jit(solution)/shard_map/psum | solution.py:12
  281.9 26.8 %copy-start.17 = (f32[128,256]{1,0:T(8,128)S(1)}, f32[128,256]{1,0:T(8,128)}, u32[]{:S(2)}) copy-start(f32[128,256]{1,0:T(8,128)} %get-tuple-element.76) | copy-start | bytes 393220
  282.0 26.8 %copy-start.18 = (f32[128,256]{1,0:T(8,128)S(1)}, f32[128,256]{1,0:T(8,128)}, u32[]{:S(2)}) copy-start(f32[128,256]{1,0:T(8,128)} %get-tuple-element.77) | copy-start | bytes 393220
  288.2 19.7 %copy-start.21 = (s32[2,2]{1,0:T(2,128)}, s32[2,2]{1,0:T(2,128)S(1)}, u32[]{:S(2)}) copy-start(s32[2,2]{1,0:T(2,128)S(1)} %get-tuple-element.401) | copy-start | bytes 52
  314.4 15.1 %copy-start.1 = (f32[1280,256]{1,0:T(8,128)}, f32[1280,256]{1,0:T(8,128)S(1)}, u32[]{:S(2)}) copy-start(f32[1280,256]{1,0:T(8,128)S(1)} %get-tuple-element.125) | copy-start | bytes 3932164
  329.6 25.4 %collective-permute-start = (f32[2560,256]{0,1:T(8,128)S(1)}, f32[2560,256]{0,1:T(8,128)}, u32[]{:S(2)}, u32[]{:S(2)}) collective-permute-start(f32[2560,256]{0,1:T(8,128)S(1)} %convolution_bitcast_fusion), channel_id=1, source_target_pairs={{0,4},{4,0},{8,12},{12,8},{16,20},{20,16},{24,28},{28,24},{1,5},{5... | collective-permute-start | bytes 7864328 | tf_op jit(solution)/shard_map/ppermute | solution.py:122
  331.2 179.2 %all-reduce.18.cloned.1.call-start = ((), (), s32[]{:S(2)}) async-start(), calls=%async_computation | async-start | bytes 2621440 | tf_op jit(solution)/shard_map/psum | solution.py:115
  332.6 0.7 copy-start.11
  354.9 4.4 copy-start.12
  358.8 121.0 %collective-permute-start.1 = (f32[2560,256]{0,1:T(8,128)}, f32[2560,256]{0,1:T(8,128)}, u32[]{:S(2)}, u32[]{:S(2)}) collective-permute-start(f32[2560,256]{0,1:T(8,128)} %add.166), channel_id=1, source_target_pairs={{0,8},{4,12},{8,0},{12,4},{16,24},{20,28},{24,16},{28,20},{1,9},{5... | collective-permute-start | bytes 7864328 | tf_op jit(solution)/shard_map/ppermute | solution.py:122
  371.6 2.5 copy-start.9
  453.8 0.7 copy-start.22
  453.8 181.3 %all-reduce.20.cloned.1.call-start = ((), (), s32[]{:S(2)}) async-start(), calls=%async_computation.1 | async-start | bytes 524288 | tf_op jit(solution)/shard_map/psum | solution.py:117
  458.6 0.7 copy-start.16
  484.2 157.6 %collective-permute-start.2 = (f32[2560,256]{0,1:T(8,128)}, f32[2560,256]{0,1:T(8,128)}, u32[]{:S(2)}, u32[]{:S(2)}) collective-permute-start(f32[2560,256]{0,1:T(8,128)} %add.167), channel_id=1, source_target_pairs={{0,16},{4,20},{8,24},{12,28},{16,0},{20,4},{24,8},{28,12},{1,17},{... | collective-permute-start | bytes 7864328 | tf_op jit(solution)/shard_map/ppermute | solution.py:122
  510.4 3.9 copy-start.2
  513.1 1.1 copy-start.7
  517.3 218.1 %all-reduce.34.cloned.1.call-start = ((), (), s32[]{:S(2)}) async-start(), calls=%async_computation.8 | async-start | bytes 2621440 | tf_op jit(solution)/shard_map/psum | solution.py:12
  641.8 6.9 copy-start.3
  673.6 5.0 copy-start
  679.8 117.7 %all-reduce.28.cloned.1.call-start = ((), (), s32[]{:S(2)}) async-start(), calls=%async_computation.5 | async-start | bytes 1048576 | tf_op jit(solution)/shard_map/psum | solution.py:12
  740.6 246.5 %all-reduce.26.cloned.1.call-start = ((), (), s32[]{:S(2)}) async-start(), calls=%async_computation.4 | async-start | bytes 5242880 | tf_op jit(solution)/shard_map/psum | solution.py:12
  833.4 27.1 %copy-start.19 = (f32[128,256]{1,0:T(8,128)S(1)}, f32[128,256]{1,0:T(8,128)}, u32[]{:S(2)}) copy-start(f32[128,256]{1,0:T(8,128)} %get-tuple-element.71) | copy-start | bytes 393220
  833.4 27.1 %copy-start.20 = (f32[128,256]{1,0:T(8,128)S(1)}, f32[128,256]{1,0:T(8,128)}, u32[]{:S(2)}) copy-start(f32[128,256]{1,0:T(8,128)} %get-tuple-element.72) | copy-start | bytes 393220
  866.2 24.4 %copy-start.4 = (f32[1280,256]{1,0:T(8,128)}, f32[1280,256]{1,0:T(8,128)S(1)}, u32[]{:S(2)}) copy-start(f32[1280,256]{1,0:T(8,128)S(1)} %get-tuple-element.130) | copy-start | bytes 3932164
  890.6 25.2 %collective-permute-start.3 = (f32[2560,256]{1,0:T(8,128)S(1)}, f32[2560,256]{1,0:T(8,128)}, u32[]{:S(2)}, u32[]{:S(2)}) collective-permute-start(f32[2560,256]{1,0:T(8,128)S(1)} %fusion.113), channel_id=1, source_target_pairs={{0,4},{4,0},{8,12},{12,8},{16,20},{20,16},{24,28},{28,24},{1,5},{5... | collective-permute-start | bytes 7864328 | tf_op jit(solution)/shard_map/ppermute | solution.py:122
  892.2 168.1 %all-reduce.22.cloned.1.call-start = ((), (), s32[]{:S(2)}) async-start(), calls=%async_computation.2 | async-start | bytes 2621440 | tf_op jit(solution)/shard_map/psum | solution.py:115
  893.4 0.7 copy-start.13
  915.7 4.4 copy-start.14
  919.5 109.8 %collective-permute-start.4 = (f32[2560,256]{1,0:T(8,128)}, f32[2560,256]{1,0:T(8,128)}, u32[]{:S(2)}, u32[]{:S(2)}) collective-permute-start(f32[2560,256]{1,0:T(8,128)} %add.169), channel_id=1, source_target_pairs={{0,8},{4,12},{8,0},{12,4},{16,24},{20,28},{24,16},{28,20},{1,9},{5... | collective-permute-start | bytes 7864328 | tf_op jit(solution)/shard_map/ppermute | solution.py:122
  932.4 2.5 copy-start.10
  1003.7 180.9 %all-reduce.24.cloned.1.call-start = ((), (), s32[]{:S(2)}) async-start(), calls=%async_computation.3 | async-start | bytes 524288 | tf_op jit(solution)/shard_map/psum | solution.py:117
  1007.8 0.7 copy-start.15
  1033.8 157.6 %collective-permute-start.5 = (f32[2560,256]{1,0:T(8,128)}, f32[2560,256]{1,0:T(8,128)}, u32[]{:S(2)}, u32[]{:S(2)}) collective-permute-start(f32[2560,256]{1,0:T(8,128)} %add.170), channel_id=1, source_target_pairs={{0,16},{4,20},{8,24},{12,28},{16,0},{20,4},{24,8},{28,12},{1,17},{... | collective-permute-start | bytes 7864328 | tf_op jit(solution)/shard_map/ppermute | solution.py:122
  1060.4 3.9 copy-start.5
  1063.1 1.1 copy-start.8
  1191.4 5.2 copy-start.6
Sparse Core Ops, SparseCore 0:
  124.8 59.0 all-reduce.35
  189.3 56.7 all-reduce.31
  331.3 94.4 all-reduce.29
  453.9 56.3 all-reduce.17
  517.4 117.7 all-reduce.19
  679.9 55.4 all-reduce.33
  740.8 56.7 all-reduce.27
  892.3 94.7 all-reduce.25
  1003.8 56.5 all-reduce.21
  1067.4 117.1 all-reduce.23
